TPU v7x, 512 devices: a whole 4x4x16 slice. The times are simulated.
512 devices in a mesh: cells: 32 (over z, core), genes: 16 (over x, y).
Axes of the slice: x: 4, y: 4, z: 16, core: 2. Of those that a mesh axis runs over, the one named last changes fastest.
Arguments:
- sketch: bfloat16 [32768, 256], P('cells'), may hold values from -6 to 6
- tiles: bfloat16 [49152, 128, 128], P(('cells', 'genes')), may hold values from -0.0546875 to 0.0546875
- tile_rows: int32 [49152], P(('cells', 'genes')), may hold values from 0 to 7, as said below
- tile_cols: int32 [49152], P(('cells', 'genes')), may hold values from 0 to 15
- tile_counts: int32 [512], P(('cells', 'genes')), may hold values from 16 to 96, as said below
Outputs:
- projected: float32 [32768, 256], P(('cells', 'genes'))
Inputs may be any that keep to these rules, and one draw needn't show every extreme that they name: Within one device's slots the pairs (tile_rows, tile_cols) are distinct. `tile_counts`: some device holds 96 tiles and the device half the cells axis away from it holds 16.
All inputs are finite; a program needn't handle non-finite values.
Results may differ from a plain program's by a relative error of at most 0.0021.
Values may be sent and summed in bfloat16 or wider, within the bound.
A program may use at most 128 MiB of HBM per device.

v0:
```python
import jax
import jax.numpy as jnp
from jax import lax
from jax.sharding import PartitionSpec as P

GENE_BLOCKS = 16


def selector(index_ids, slot_live, width):
    hits = (index_ids[:, None] == jnp.arange(width, dtype=jnp.int32)[None, :]).astype(jnp.float32)
    return hits * slot_live[:, None]


def local(sketch, tiles, tile_rows, tile_cols, tile_counts):
    tile_size = tiles.shape[1]
    sketch_width = sketch.shape[1]
    slot_total = tiles.shape[0]
    row_blocks = sketch.shape[0] // tile_size
    sketch_blocks = sketch.reshape(row_blocks, tile_size, sketch_width)
    slot_live = (jnp.arange(slot_total, dtype=jnp.int32) < tile_counts[0]).astype(jnp.float32)
    col_select = selector(tile_cols, slot_live, GENE_BLOCKS)
    row_select = selector(tile_rows, slot_live, row_blocks)
    picked_rows = sketch_blocks[tile_rows]
    first_terms = jnp.einsum("ski,skr->sir", tiles, picked_rows, preferred_element_type=jnp.float32)
    gene_acc = jnp.einsum("sg,sir->gir", col_select, first_terms, precision=lax.Precision.HIGHEST)
    gene_cast = lax.psum(gene_acc, "cells").astype(jnp.bfloat16)
    picked_genes = gene_cast[tile_cols]
    second_terms = jnp.einsum(
        "sik,skr->sir", tiles, picked_genes, preferred_element_type=jnp.float32
    )
    cell_acc = jnp.einsum("sb,sir->bir", row_select, second_terms, precision=lax.Precision.HIGHEST)
    return lax.psum_scatter(
        cell_acc.reshape(row_blocks * tile_size, sketch_width),
        "genes",
        scatter_dimension=0,
        tiled=True,
    )


def solution(mesh):
    in_specs = (
        P("cells", None),
        P(("cells", "genes"), None, None),
        P(("cells", "genes")),
        P(("cells", "genes")),
        P(("cells", "genes")),
    )
    out_specs = P(("cells", "genes"), None)
    return jax.shard_map(local, mesh=mesh, in_specs=in_specs, out_specs=out_specs, check_vma=False)
```

profile of v0, /device:TPU:2, one launch (start us, length us, event | category | flops | bytes accessed | tf_op | source)
XLA Modules:
  0.0 301.6 jit_solution(11839636375966423922)
XLA Ops:
  6.5 0.0 copy-start
  6.5 0.0 reduce-scatter.2.cloned.1.call-start
  7.4 0.8 compare_select_fusion.1
  8.2 7.0 %gather_fusion = bf16[96,128,256]{2,1,0:T(8,128)(2,1)} fusion(bf16[8,128,256]{2,1,0:T(8,128)(2,1)} %bitcast.20, s32[1024]{0:T(1024)S(1)} %pad_clamp_fusion.1), kind=kCustom, calls=%fused_computation | custom fusion | bytes 12583296 | tf_op jit(solution)/shard_map/gather | solution.py:23
  15.1 0.0 copy-done
  15.1 9.2 %convolution_bitcast_fusion = f32[96,128,256]{1,2,0:T(8,128)} fusion(bf16[96,128,256]{2,1,0:T(8,128)(2,1)} %gather_fusion, bf16[96,128,128]{2,1,0:T(8,128)(2,1)S(1)} %copy-done), kind=kOutput, calls=%fused_computation.4 | convolution fusion | flops 805306368 | bytes 22020096 | tf_op jit(solution)/shard_map/ski,skr->sir/dot_general | solution.py:24
  24.3 0.0 copy-start.1
  24.3 12.7 %copy.7 = f32[96,128,256]{2,0,1:T(8,128)} copy(f32[96,128,256]{1,2,0:T(8,128)} %convolution_bitcast_fusion) | data formatting | bytes 25165824 | tf_op jit(solution)/shard_map/ski,skr->sir/dot_general | solution.py:24
  37.0 0.0 copy-done.1
  37.0 9.1 %fusion.2 = f32[16,128,256]{2,0,1:T(8,128)S(1)} fusion(f32[96,128,256]{2,0,1:T(8,128)} %copy.7, f32[96]{0:T(128)S(1)} %compare_convert_fusion, s32[96]{0:T(128)S(1)} %copy-done.1), kind=kOutput, calls=%fused_computation.5 | convolution fusion | flops 603982848 | bytes 14680832 | tf_op jit(solution)/shard_map/sg,sir->gir/dot_general | solution.py:25
  46.1 2.6 copy.8
  48.7 122.1 %all-reduce.1 = bf16[16,128,256]{2,1,0:T(8,128)(2,1)} all-reduce(f32[16,128,256]{2,1,0:T(8,128)} %copy.8), channel_id=1, replica_groups=mesh['cells'=32,'genes'=16] {'cells'}, use_global_device_ids=true, to_apply=%region_0.0 | all-reduce | flops 524288 | bytes 3145728 | tf_op jit(solution)/shard_map/psum | solution.py:26
  170.8 7.2 %gather_fusion.1 = bf16[96,128,256]{2,1,0:T(8,128)(2,1)} fusion(bf16[16,128,256]{2,1,0:T(8,128)(2,1)} %all-reduce.1, s32[1024]{0:T(1024)S(1)} %pad_clamp_fusion), kind=kCustom, calls=%fused_computation.1 | custom fusion | bytes 12583296 | tf_op jit(solution)/shard_map/gather | solution.py:27
  177.9 9.2 %fusion.15 = f32[96,256,128]{2,1,0:T(8,128)} fusion(bf16[96,128,256]{2,1,0:T(8,128)(2,1)} %gather_fusion.1, bf16[96,128,128]{2,1,0:T(8,128)(2,1)S(1)} %copy-done), kind=kOutput, calls=%fused_computation.25 | convolution fusion | flops 805306368 | bytes 22020096 | tf_op jit(solution)/shard_map/sik,skr->sir/dot_general | solution.py:28
  187.1 0.0 copy-start.2
  187.1 12.7 %copy.9 = f32[96,256,128]{1,0,2:T(8,128)} copy(f32[96,256,128]{2,1,0:T(8,128)} %fusion.15) | data formatting | bytes 25165824 | tf_op jit(solution)/shard_map/sik,skr->sir/dot_general | solution.py:28
  199.8 0.0 copy-done.2
  199.8 8.9 %fusion = f32[8,128,256]{2,0,1:T(8,128)S(1)} fusion(f32[96,256,128]{1,0,2:T(8,128)} %copy.9, f32[96]{0:T(128)S(1)} %compare_convert_fusion, s32[96]{0:T(128)S(1)} %copy-done.2), kind=kOutput, calls=%fused_computation.2 | convolution fusion | flops 301991424 | bytes 13632256 | tf_op jit(solution)/shard_map/sb,sir->bir/dot_general | solution.py:31
  208.7 1.3 copy.6
  210.0 0.0 reduce-scatter.2.cloned.1.call-update
  210.1 84.7 %reduce-scatter.2.cloned.1.call-done = f32[64,256]{1,0:T(8,128)} async-done(((f32[1024,256]{1,0:T(8,128)}), f32[64,256]{1,0:T(8,128)}) %reduce-scatter.2.cloned.1.call-update) | async-done | bytes 65552 | tf_op jit(solution)/shard_map/reduce_scatter | solution.py:32
  (4 shorter events, 0.0 us)
Async XLA Ops:
  6.5 8.6 %copy-start = (bf16[96,128,128]{2,1,0:T(8,128)(2,1)S(1)}, bf16[96,128,128]{2,1,0:T(8,128)(2,1)}, u32[]{:S(2)}) copy-start(bf16[96,128,128]{2,1,0:T(8,128)(2,1)} %param.6) | copy-start | bytes 9437188
  6.5 288.2 %reduce-scatter.2.cloned.1.call-start = ((), (), s32[]{:S(2)}) async-start(), calls=%async_computation.1 | async-start | bytes 1114112 | tf_op jit(solution)/shard_map/reduce_scatter | solution.py:32
  24.3 12.7 %copy-start.1 = (s32[96]{0:T(128)S(1)}, s32[96]{0:T(128)}, u32[]{:S(2)}) copy-start(s32[96]{0:T(128)} %param.8) | copy-start | bytes 1156
  187.1 12.7 %copy-start.2 = (s32[96]{0:T(128)S(1)}, s32[96]{0:T(128)}, u32[]{:S(2)}) copy-start(s32[96]{0:T(128)} %param.7) | copy-start | bytes 1156
Sparse Core Ops, SparseCore 0:
  210.2 84.5 reduce-scatter.1
where the time goes:
time: 302 us
  blocking collectives  122 us (40%)
  waiting for transfers between devices  84.7 us (28%)
  local copies, waits for them, and re-layouts  43.4 us (14%)
  matrix products  36.3 us (12%)
  between operations  14.2 us (5%)
    psum x1, blocking collectives, local(): gene_cast = lax.psum(gene_acc, 'cells').astype(jnp.bfloat16)  122 us
    reduce_scatter x1, waiting for transfers between devices, local(): lax.psum_scatter(cell_acc.reshape(row_blocks * tile_size, sketch_width),...  84.7 us
    dot_general x1, local copies, waits for them, and re-layouts, local(): jnp.einsum('sik,skr->sir', tiles, picked_genes, preferred_element_type=jn...  12.7 us
    dot_general x1, local copies, waits for them, and re-layouts, local(): jnp.einsum('ski,skr->sir', tiles, picked_rows, preferred_element_type=jnp...  12.7 us
    dot_general x1, matrix products, local(): jnp.einsum('sik,skr->sir', tiles, picked_genes, preferred_element_type=jn...  9.19 us
    dot_general x1, matrix products, local(): jnp.einsum('ski,skr->sir', tiles, picked_rows, preferred_element_type=jnp...  9.19 us
    dot_general x1, matrix products, local(): jnp.einsum('sg,sir->gir', col_select, first_terms, precision=lax.Precisio...  9.05 us
    dot_general x1, matrix products, local(): jnp.einsum('sb,sir->bir', row_select, second_terms, precision=lax.Precisi...  8.9 us
  transfers between devices with their start and end apart: 1, of which 1 were waited for; matrix products, arithmetic and copies ran while one was open for 0% of the time, Pallas kernels for 0%

commit v1 on v0

--- a/solution.py
+++ b/solution.py
@@ -1,9 +1,17 @@
+import functools
 import jax
 import jax.numpy as jnp
 from jax import lax
 from jax.sharding import PartitionSpec as P
 
 GENE_BLOCKS = 16
+
+
+def supply_samples_all_over_axis(x_in, mesh_dim):
+    return jnp.sum(lax.all_gather(x_in, axis_name=mesh_dim), 0)
+
+
+keep_up_series_all_on_mesh = functools.partial(supply_samples_all_over_axis, mesh_dim="cells")
 
 
 def selector(index_ids, slot_live, width):
@@ -23,7 +31,7 @@
     picked_rows = sketch_blocks[tile_rows]
     first_terms = jnp.einsum("ski,skr->sir", tiles, picked_rows, preferred_element_type=jnp.float32)
     gene_acc = jnp.einsum("sg,sir->gir", col_select, first_terms, precision=lax.Precision.HIGHEST)
-    gene_cast = lax.psum(gene_acc, "cells").astype(jnp.bfloat16)
+    gene_cast = keep_up_series_all_on_mesh(gene_acc).astype(jnp.bfloat16)
     picked_genes = gene_cast[tile_cols]
     second_terms = jnp.einsum(
         "sik,skr->sir", tiles, picked_genes, preferred_element_type=jnp.float32

time: 302 us -> 569 us (1.88)
  waiting for transfers between devices: 84.7 us -> 451 us
  blocking collectives: 122 us -> 0 us
  other arithmetic: 0.82 us -> 22.8 us
    all_gather x0 -> x1, waiting for transfers between devices: none -> 364 us  [supply_samples_all_over_axis(): return jnp.sum(lax.all_gather(x_in, axis_name=mesh_dim), 0)]
    psum x1 -> x0, blocking collectives: 122 us -> none  [local(): gene_cast = lax.psum(gene_acc, 'cells').astype(jnp.bfloat16)]
    reduce_sum x0 -> x1, other arithmetic: none -> 22 us  [supply_samples_all_over_axis(): return jnp.sum(lax.all_gather(x_in, axis_name=mesh_dim), 0)]
  transfers between devices with their start and end apart: 1 -> 2, of which waited for: 1 -> 2; matrix products, arithmetic and copies ran while one was open for 0% -> 0% of each run, Pallas kernels for 0% -> 0%
where the time goes in v1:
time: 569 us
  waiting for transfers between devices  451 us (79%)
  local copies, waits for them, and re-layouts  43.3 us (8%)
  matrix products  36.9 us (6%)
  other arithmetic  22.8 us (4%)
  between operations  14.2 us (2%)
    all_gather x1, waiting for transfers between devices, supply_samples_all_over_axis(): return jnp.sum(lax.all_gather(x_in, axis_name=mesh_dim), 0)  364 us
    reduce_scatter x1, waiting for transfers between devices, local(): lax.psum_scatter(cell_acc.reshape(row_blocks * tile_size, sketch_width),...  87 us
    reduce_sum x1, other arithmetic, supply_samples_all_over_axis(): return jnp.sum(lax.all_gather(x_in, axis_name=mesh_dim), 0)  22 us
    dot_general x1, local copies, waits for them, and re-layouts, local(): jnp.einsum('ski,skr->sir', tiles, picked_rows, preferred_element_type=jnp...  12.7 us
    dot_general x1, local copies, waits for them, and re-layouts, local(): jnp.einsum('sik,skr->sir', tiles, picked_genes, preferred_element_type=jn...  12.7 us
  transfers between devices with their start and end apart: 2, of which 2 were waited for; matrix products, arithmetic and copies ran while one was open for 0% of the time, Pallas kernels for 0%

profile of v1, /device:TPU:2, one launch (start us, length us, event | category | flops | bytes accessed | tf_op | source)
XLA Modules:
  0.0 568.9 jit_solution(4233494310680509801)
XLA Ops:
  6.5 0.0 copy-start
  6.5 0.0 all-gather.3.cloned.1.call-start
  7.4 0.8 compare_select_fusion.1
  8.2 6.9 %gather_fusion = bf16[96,128,256]{2,1,0:T(8,128)(2,1)} fusion(bf16[8,128,256]{2,1,0:T(8,128)(2,1)} %bitcast.21, s32[1024]{0:T(1024)S(1)} %pad_clamp_fusion.1), kind=kCustom, calls=%fused_computation | custom fusion | bytes 12583296 | tf_op jit(solution)/shard_map/gather | solution.py:31
  15.1 0.0 copy-done
  15.1 9.2 %convolution_bitcast_fusion.1 = f32[96,128,256]{1,2,0:T(8,128)} fusion(bf16[96,128,256]{2,1,0:T(8,128)(2,1)} %gather_fusion, bf16[96,128,128]{2,1,0:T(8,128)(2,1)S(1)} %copy-done), kind=kOutput, calls=%fused_computation.3 | convolution fusion | flops 805306368 | bytes 22020096 | tf_op jit(solution)/shard_map/ski,skr->sir/dot_general | solution.py:32
  24.3 0.0 copy-start.1
  24.3 12.7 %copy.12 = f32[96,128,256]{2,0,1:T(8,128)} copy(f32[96,128,256]{1,2,0:T(8,128)} %convolution_bitcast_fusion.1) | data formatting | bytes 25165824 | tf_op jit(solution)/shard_map/ski,skr->sir/dot_general | solution.py:32
  37.0 0.0 copy-done.1
  37.0 9.6 %fusion = f32[16,128,256]{2,0,1:T(8,128)} fusion(f32[96,128,256]{2,0,1:T(8,128)} %copy.12, f32[96]{0:T(128)S(1)} %compare_convert_fusion, s32[96]{0:T(128)S(1)} %copy-done.1), kind=kOutput, calls=%fused_computation.5 | convolution fusion | flops 603982848 | bytes 14680832 | tf_op jit(solution)/shard_map/sg,sir->gir/dot_general | solution.py:33
  46.6 0.0 all-gather.3.cloned.1.call-update
  46.6 0.2 reduce-scatter.2.cloned.1.call-start
  46.9 364.4 %all-gather.3.cloned.1.call-done = f32[512,128,256]{2,0,1:T(8,128)} async-done(((f32[16,128,256]{2,0,1:T(8,128)}), f32[512,128,256]{2,0,1:T(8,128)}) %all-gather.3.cloned.1.call-update) | async-done | bytes 67108880 | tf_op jit(solution)/shard_map/all_gather | solution.py:11
  411.3 22.0 %reduce_sum.9 = bf16[16,128,256]{2,0,1:T(8,128)(2,1)} reduce(f32[32,16,128,256]{3,1,0,2:T(8,128)} %bitcast.5, f32[]{:T(128)} %constant.2.clone.1), dimensions={0}, to_apply=%region_0.0 | reduce | flops 16252928 | bytes 68157440 | tf_op jit(solution)/shard_map/reduce_sum | solution.py:11
  433.3 2.5 copy.20
  435.8 7.1 %gather_fusion.1 = bf16[96,128,256]{2,1,0:T(8,128)(2,1)} fusion(bf16[16,128,256]{2,1,0:T(8,128)(2,1)} %copy.20, s32[1024]{0:T(1024)S(1)} %pad_clamp_fusion), kind=kCustom, calls=%fused_computation.1 | custom fusion | bytes 12583296 | tf_op jit(solution)/shard_map/gather | solution.py:35
  442.9 9.2 %convolution_bitcast_fusion = f32[96,128,256]{1,2,0:T(8,128)} fusion(bf16[96,128,256]{2,1,0:T(8,128)(2,1)} %gather_fusion.1, bf16[96,128,128]{2,1,0:T(8,128)(2,1)S(1)} %copy-done), kind=kOutput, calls=%fused_computation.2 | convolution fusion | flops 805306368 | bytes 22020096 | tf_op jit(solution)/shard_map/sik,skr->sir/dot_general | solution.py:36
  452.1 0.0 copy-start.2
  452.1 12.7 %copy.15 = f32[96,128,256]{2,0,1:T(8,128)} copy(f32[96,128,256]{1,2,0:T(8,128)} %convolution_bitcast_fusion) | data formatting | bytes 25165824 | tf_op jit(solution)/shard_map/sik,skr->sir/dot_general | solution.py:36
  464.8 0.0 copy-done.2
  464.8 8.9 %fusion.3 = f32[8,128,256]{2,0,1:T(8,128)S(1)} fusion(f32[96,128,256]{2,0,1:T(8,128)} %copy.15, f32[96]{0:T(128)S(1)} %compare_convert_fusion, s32[96]{0:T(128)S(1)} %copy-done.2), kind=kOutput, calls=%fused_computation.11 | convolution fusion | flops 301991424 | bytes 13632256 | tf_op jit(solution)/shard_map/sb,sir->bir/dot_general | solution.py:39
  473.7 1.3 copy.16
  475.0 0.0 reduce-scatter.2.cloned.1.call-update
  475.1 87.0 %reduce-scatter.2.cloned.1.call-done = f32[64,256]{1,0:T(8,128)} async-done(((f32[1024,256]{1,0:T(8,128)}), f32[64,256]{1,0:T(8,128)}) %reduce-scatter.2.cloned.1.call-update) | async-done | bytes 65552 | tf_op jit(solution)/shard_map/reduce_scatter | solution.py:40
  (4 shorter events, 0.0 us)
Async XLA Ops:
  6.5 8.6 %copy-start = (bf16[96,128,128]{2,1,0:T(8,128)(2,1)S(1)}, bf16[96,128,128]{2,1,0:T(8,128)(2,1)}, u32[]{:S(2)}) copy-start(bf16[96,128,128]{2,1,0:T(8,128)(2,1)} %param.6) | copy-start | bytes 9437188
  6.5 404.8 %all-gather.3.cloned.1.call-start = ((), (), s32[]{:S(2)}) async-start(), calls=%async_computation.2 | async-start | bytes 69206016 | tf_op jit(solution)/shard_map/all_gather | solution.py:11
  24.3 12.7 %copy-start.1 = (s32[96]{0:T(128)S(1)}, s32[96]{0:T(128)}, u32[]{:S(2)}) copy-start(s32[96]{0:T(128)} %param.8) | copy-start | bytes 1156
  46.6 515.4 %reduce-scatter.2.cloned.1.call-start = ((), (), s32[]{:S(2)}) async-start(), calls=%async_computation.1 | async-start | bytes 1114112 | tf_op jit(solution)/shard_map/reduce_scatter | solution.py:40
  452.1 12.7 %copy-start.2 = (s32[96]{0:T(128)S(1)}, s32[96]{0:T(128)}, u32[]{:S(2)}) copy-start(s32[96]{0:T(128)} %param.7) | copy-start | bytes 1156
Sparse Core Ops, SparseCore 0:
  46.8 364.5 all-gather.2
  475.2 86.8 reduce-scatter.1
